TPU v7x, 32 devices: a whole 2x2x4 slice. The times are simulated.
32 devices in a mesh: dp: 2 (over x), ctx: 16 (over z, y, core).
Axes of the slice: x: 2, y: 2, z: 4, core: 2. Of those that a mesh axis runs over, the one named last changes fastest.
Arguments:
- token_ids: int32 [2, 2048], P('dp', 'ctx'), may hold values from 0 to 7
- queries: bfloat16 [2, 2048, 4096], P('dp', 'ctx'), may hold values from -6 to 6
- gated_values: bfloat16 [2, 2048, 4096], P('dp', 'ctx'), may hold values from -6 to 6
- out_grad: bfloat16 [2, 2048, 4096], P('dp', 'ctx'), may hold values from -6 to 6
- filters: bfloat16 [4096, 128], P('ctx'), may hold values from -0.5 to 0.5
Outputs:
- value_grad: bfloat16 [2, 2048, 4096], P('dp', 'ctx')
- filter_grad: float32 [4096, 128], P('ctx')
Inputs may be any that keep to these rules, and one draw needn't show every extreme that they name: `token_ids`: ids 0 to 3 are upper-case bases, 4 to 7 lower-case bases.
All inputs are finite; a program needn't handle non-finite values.
Results may differ from a plain program's by a relative error of at most 0.0049.
Values may be sent and summed in bfloat16 or wider, within the bound.
No kernel may reach another device: no remote copies, remote signals or barrier semaphores. Data moves between devices by JAX's collectives and lax.ppermute only.
A program may use at most 64 MiB of HBM per device.

v0:
```python
import jax
import jax.numpy as jnp
from jax import lax
from jax.sharding import PartitionSpec as P


def shifted(x, axis, by):
    length = lax.axis_size(axis)
    pairs = [(i, i + by) for i in range(length) if 0 <= i + by < length]
    return lax.ppermute(x, axis, pairs)


def correlate(signal, kernel):
    channels = signal.shape[2]
    return lax.conv_general_dilated(
        signal,
        kernel[:, None, :],
        (1,),
        "VALID",
        dimension_numbers=("NWC", "WIO", "NWC"),
        feature_group_count=channels,
        preferred_element_type=jnp.float32,
    )


def body(token_ids, queries, gated_values, out_grad, filters):
    weight = jnp.where(token_ids < 4, 1.0, 0.1).astype(jnp.float32)
    cotangent = (
        weight[:, :, None] * out_grad.astype(jnp.float32) * queries.astype(jnp.float32)
    ).astype(jnp.bfloat16)
    tap_count = filters.shape[1]
    token_total = lax.axis_size("dp") * lax.axis_size("ctx") * queries.shape[1]
    factor_tok = float(token_total) ** (-0.5)
    next_part = shifted(cotangent[:, : tap_count - 1], "ctx", -1)
    signal = jnp.concatenate([cotangent, next_part], axis=1)
    all_filters = lax.all_gather(filters, "ctx", axis=0, tiled=True)
    value_grad = correlate(signal, all_filters.T).astype(jnp.bfloat16)
    values_wide = gated_values[0]
    local_taps = lax.psum_scatter(
        correlate(signal, values_wide)[0].T * factor_tok, "ctx", scatter_dimension=0, tiled=True
    )
    filter_grad = lax.psum(local_taps, "dp")
    return (value_grad, filter_grad)


def solution(mesh):
    return jax.shard_map(
        body,
        mesh=mesh,
        in_specs=(
            P("dp", "ctx"),
            P("dp", "ctx", None),
            P("dp", "ctx", None),
            P("dp", "ctx", None),
            P("ctx", None),
        ),
        out_specs=(P("dp", "ctx", None), P("ctx", None)),
        check_vma=False,
    )
```

profile of v0, /device:TPU:0, one launch (start us, length us, event | category | flops | bytes accessed | tf_op | source)
XLA Modules:
  0.0 201.7 jit_solution(6966847847205426817)
XLA Ops:
  7.2 0.0 copy-start
  7.2 0.0 reduce-scatter.2.cloned.1.call-start
  7.2 0.7 fusion.4
  8.0 2.0 multiply_convert_fusion
  10.0 1.3 collective-permute-start
  11.3 3.3 %collective-permute-done = bf16[1,127,4096]{2,1,0:T(8,128)(2,1)S(1)} collective-permute-done((bf16[1,127,4096]{2,1,0:T(8,128)(2,1)S(1)}, bf16[1,127,4096]{2,1,0:T(8,128)(2,1)S(1)}, u32[]{:S(2)}, u32[]{:S(2)}) %collective-permute-start) | collective-permute-done | bytes 1040416 | tf_op jit(solution)/shard_map/ppermute | solution.py:10
  14.5 0.2 pad_maximum_fusion
  14.7 0.0 copy-done
  14.7 30.5 %convolution_multiply_fusion = f32[1,128,4096]{2,0,1:T(1,128)S(1)} fusion(bf16[1,255,4096]{2,1,0:T(8,128)(2,1)S(1)} %pad_maximum_fusion, bf16[128,1,4096]{2,0,1:T(8,128)(2,1)S(1)} %bitcast.12), kind=kOutput, calls=%fused_computation.1 | convolution fusion | flops 134742016 | bytes 5234688 | tf_op jit(solution)/shard_map/conv_general_dilated | solution.py:15
  45.3 3.0 %copy.46 = f32[1,128,4096]{2,1,0:T(8,128)} copy(f32[1,128,4096]{2,0,1:T(1,128)S(1)} %convolution_multiply_fusion) | data formatting | bytes 4194304
  48.3 0.0 copy-start.1
  48.3 0.0 reduce-scatter.2.cloned.1.call-update
  48.3 0.0 all-gather.2.cloned.1.call-start
  48.4 0.8 copy-done.1
  49.1 0.7 copy.29
  49.9 0.0 all-gather.2.cloned.1.call-update
  49.9 0.0 all-reduce.2.cloned.1.call-start
  49.9 74.0 %reduce-scatter.2.cloned.1.call-done = f32[256,128]{0,1:T(8,128)} async-done(((f32[4096,128]{0,1:T(8,128)}), f32[256,128]{0,1:T(8,128)}) %reduce-scatter.2.cloned.1.call-update) | async-done | bytes 131088 | tf_op jit(solution)/shard_map/reduce_scatter | solution.py:39
  124.0 0.0 all-reduce.2.cloned.1.call-update
  124.0 38.3 %all-gather.2.cloned.1.call-done = bf16[4096,128]{0,1:T(8,128)(2,1)} async-done(((bf16[256,128]{0,1:T(8,128)(2,1)}), bf16[4096,128]{0,1:T(8,128)(2,1)}) %all-gather.2.cloned.1.call-update) | async-done | bytes 1048592 | tf_op jit(solution)/shard_map/all_gather | solution.py:36
  162.3 29.1 %convolution_convert_fusion = bf16[1,128,4096]{2,0,1:T(2,128)(2,1)S(1)} fusion(bf16[1,255,4096]{2,1,0:T(8,128)(2,1)S(1)} %pad_maximum_fusion, bf16[128,1,4096]{2,0,1:T(8,128)(2,1)} %bitcast.15), kind=kOutput, calls=%fused_computation | convolution fusion | flops 134742016 | bytes 4186112 | tf_op jit(solution)/shard_map/conv_general_dilated | solution.py:15
  191.4 2.1 %copy.34 = bf16[1,128,4096]{2,1,0:T(8,128)(2,1)} copy(bf16[1,128,4096]{2,0,1:T(2,128)(2,1)S(1)} %convolution_convert_fusion) | data formatting | bytes 2097152
  193.5 0.0 all-reduce.2.cloned.1.call-done
  193.5 1.7 copy.35
Async XLA Ops:
  7.2 7.6 %copy-start = (bf16[1,128,4096]{2,1,0:T(8,128)(2,1)S(1)}, bf16[1,128,4096]{2,1,0:T(8,128)(2,1)}, u32[]{:S(2)}) copy-start(bf16[1,128,4096]{2,1,0:T(8,128)(2,1)} %param.7) | copy-start | bytes 3145732
  7.2 116.8 %reduce-scatter.2.cloned.1.call-start = ((), (), s32[]{:S(2)}) async-start(), calls=%async_computation.2 | async-start | bytes 2228224 | tf_op jit(solution)/shard_map/reduce_scatter | solution.py:39
  10.0 4.6 %collective-permute-start = (bf16[1,127,4096]{2,1,0:T(8,128)(2,1)S(1)}, bf16[1,127,4096]{2,1,0:T(8,128)(2,1)S(1)}, u32[]{:S(2)}, u32[]{:S(2)}) collective-permute-start(bf16[1,127,4096]{2,1,0:T(8,128)(2,1)S(1)} %bitcast.14), channel_id=1, source_target_pairs={{1,0},{2,1},{3,2},{4,3},{5,4},{6,5},{7,6},{8,7},{9,8},{10,9},{11,1... | collective-permute-start | bytes 3121160 | tf_op jit(solution)/shard_map/ppermute | solution.py:10
  48.3 0.8 copy-start.1
  48.3 114.0 %all-gather.2.cloned.1.call-start = ((), (), s32[]{:S(2)}) async-start(), calls=%async_computation.1 | async-start | bytes 1114112 | tf_op jit(solution)/shard_map/all_gather | solution.py:36
  49.9 143.6 %all-reduce.2.cloned.1.call-start = ((), (), s32[]{:S(2)}) async-start(), calls=%async_computation.3 | async-start | bytes 262144 | tf_op jit(solution)/shard_map/psum | solution.py:42
Sparse Core Ops, SparseCore 0:
  48.4 75.4 reduce-scatter.1
  126.7 35.5 all-gather.1
  164.6 21.1 all-reduce.1
where the time goes:
time: 202 us
  waiting for transfers between devices  116 us (57%)
  matrix products  59.6 us (30%)
  between operations  13.8 us (7%)
  local copies, waits for them, and re-layouts  8.28 us (4%)
  other arithmetic  2.94 us (1%)
    reduce_scatter x1, waiting for transfers between devices, body(): lax.psum_scatter(correlate(signal, values_wide)[0].T * factor_tok, 'ctx',...  74 us
    conv_general_dilated x2, matrix products, correlate(): lax.conv_general_dilated(signal, kernel[:, None, :], (1,), 'VALID', dimen...  59.6 us
    all_gather x1, waiting for transfers between devices, body(): all_filters = lax.all_gather(filters, 'ctx', axis=0, tiled=True)  38.3 us
    unnamed x8, local copies, waits for them, and re-layouts  8.28 us
  transfers between devices with their start and end apart: 4, of which 3 were waited for; matrix products, arithmetic and copies ran while one was open for 16% of the time, Pallas kernels for 0%

commit v1 on v0

--- a/solution.py
+++ b/solution.py
@@ -33,7 +33,16 @@
     factor_tok = float(token_total) ** (-0.5)
     next_part = shifted(cotangent[:, : tap_count - 1], "ctx", -1)
     signal = jnp.concatenate([cotangent, next_part], axis=1)
-    all_filters = lax.all_gather(filters, "ctx", axis=0, tiled=True)
+    size, position, rows = (lax.axis_size("ctx"), lax.axis_index("ctx"), filters.shape[0])
+    forward = [(i_2, (i_2 + 1) % size) for i_2 in range(size)]
+    out = jnp.zeros((*filters.shape[:0], size * rows, *filters.shape[0 + 1 :]), filters.dtype)
+    block = filters
+    for hop in range(size):
+        owner = (position - hop) % size
+        out = lax.dynamic_update_slice_in_dim(out, block, owner * rows, axis=0)
+        if hop < size - 1:
+            block = lax.ppermute(block, "ctx", forward)
+    all_filters = out
     value_grad = correlate(signal, all_filters.T).astype(jnp.bfloat16)
     values_wide = gated_values[0]
     local_taps = lax.psum_scatter(

time: 202 us -> 198 us (0.980)
  waiting for transfers between devices: 116 us -> 87.4 us
  starting transfers between devices: 1.41 us -> 14.8 us
  local copies, waits for them, and re-layouts: 8.28 us -> 18.8 us
    ppermute x0 -> x15, waiting for transfers between devices: none -> 84.1 us  [body(): block = lax.ppermute(block, 'ctx', forward)]
    reduce_scatter x1, waiting for transfers between devices: 74 us -> 0.01 us  [body(): lax.psum_scatter(correlate(signal, values_wide)[0].T * factor_tok, 'ctx',...]
    all_gather x1 -> x0, waiting for transfers between devices: 38.3 us -> none  [body(): all_filters = lax.all_gather(filters, 'ctx', axis=0, tiled=True)]
    ppermute x0 -> x15, starting transfers between devices: none -> 13.4 us  [body(): block = lax.ppermute(block, 'ctx', forward)]
    dynamic_update_slice x0 -> x16, local copies, waits for them, and re-layouts: none -> 10.1 us  [body(): out = lax.dynamic_update_slice_in_dim(out, block, owner * rows, axis=0)]
  transfers between devices with their start and end apart: 4 -> 18, of which waited for: 3 -> 15; matrix products, arithmetic and copies ran while one was open for 16% -> 22% of each run, Pallas kernels for 0% -> 0%
where the time goes in v1:
time: 198 us
  waiting for transfers between devices  87.4 us (44%)
  matrix products  59.6 us (30%)
  local copies, waits for them, and re-layouts  18.8 us (9%)
  starting transfers between devices  14.8 us (7%)
  between operations  14.1 us (7%)
  other arithmetic  2.94 us (1%)
    ppermute x15, waiting for transfers between devices, body(): block = lax.ppermute(block, 'ctx', forward)  84.1 us
    conv_general_dilated x2, matrix products, correlate(): lax.conv_general_dilated(signal, kernel[:, None, :], (1,), 'VALID', dimen...  59.6 us
    ppermute x15, starting transfers between devices, body(): block = lax.ppermute(block, 'ctx', forward)  13.4 us
    dynamic_update_slice x16, local copies, waits for them, and re-layouts, body(): out = lax.dynamic_update_slice_in_dim(out, block, owner * rows, axis=0)  10.1 us
    unnamed x8, local copies, waits for them, and re-layouts  7.63 us
  transfers between devices with their start and end apart: 18, of which 15 were waited for; matrix products, arithmetic and copies ran while one was open for 22% of the time, Pallas kernels for 0%

profile of v1, /device:TPU:0, one launch (start us, length us, event | category | flops | bytes accessed | tf_op | source)
XLA Modules:
  0.0 197.7 jit_solution(5517771045459071581)
XLA Ops:
  7.2 0.0 copy-start
  7.2 0.0 reduce-scatter.2.cloned.1.call-start
  7.2 0.7 fusion.4
  8.0 2.0 %multiply_convert_fusion = bf16[1,128,4096]{2,1,0:T(8,128)(2,1)S(1)} fusion(bf16[1,128,4096]{2,1,0:T(8,128)(2,1)} %param.6, bf16[1,128,4096]{2,1,0:T(8,128)(2,1)} %param.8, f32[128]{0:T(128)S(1)} %fusion.4), kind=kLoop, calls=%fused_computation.8 | loop fusion | flops 2621440 | bytes 3146240 | tf_op jit(solution)/shard_map/convert_element_type | solution.py:30
  10.0 1.3 collective-permute-start
  11.3 3.3 %collective-permute-done = bf16[1,127,4096]{2,1,0:T(8,128)(2,1)S(1)} collective-permute-done((bf16[1,127,4096]{2,1,0:T(8,128)(2,1)S(1)}, bf16[1,127,4096]{2,1,0:T(8,128)(2,1)S(1)}, u32[]{:S(2)}, u32[]{:S(2)}) %collective-permute-start) | collective-permute-done | bytes 1040416 | tf_op jit(solution)/shard_map/ppermute | solution.py:10
  14.5 0.2 pad_maximum_fusion
  14.7 30.5 %convolution_multiply_fusion = f32[1,128,4096]{2,0,1:T(1,128)S(1)} fusion(bf16[1,255,4096]{2,1,0:T(8,128)(2,1)S(1)} %pad_maximum_fusion, bf16[128,1,4096]{2,0,1:T(8,128)(2,1)S(1)} %bitcast.12), kind=kOutput, calls=%fused_computation.1 | convolution fusion | flops 134742016 | bytes 5234688 | tf_op jit(solution)/shard_map/conv_general_dilated | solution.py:15
  45.3 3.0 %copy.64 = f32[1,128,4096]{2,1,0:T(8,128)} copy(f32[1,128,4096]{2,0,1:T(1,128)S(1)} %convolution_multiply_fusion) | data formatting | bytes 4194304
  48.3 0.0 reduce-scatter.2.cloned.1.call-update
  48.3 0.0 all-reduce.2.cloned.1.call-start
  48.3 0.8 copy-done.1
  49.1 0.1 copy.46
  49.2 13.0 %collective-permute-start.1 = (bf16[256,128]{0,1:T(8,128)(2,1)S(1)}, bf16[256,128]{0,1:T(8,128)(2,1)S(1)}, u32[]{:S(2)}, u32[]{:S(2)}) collective-permute-start(bf16[256,128]{0,1:T(8,128)(2,1)S(1)} %copy.46), channel_id=1, source_target_pairs={{0,1},{1,2},{2,3},{3,4},{4,5},{5,6},{6,7},{7,8},{8,9},{9,10},{10,1... | collective-permute-start | bytes 196616 | tf_op jit(solution)/shard_map/ppermute | solution.py:44
  62.2 1.1 broadcast_in_dim.17
  63.3 0.6 constant_dynamic-update-slice_fusion.15
  63.9 0.0 collective-permute-done.1
  63.9 0.4 collective-permute-start.2
  64.3 0.6 constant_dynamic-update-slice_fusion.14
  64.9 5.4 %collective-permute-done.2 = bf16[256,128]{0,1:T(8,128)(2,1)S(1)} collective-permute-done((bf16[256,128]{0,1:T(8,128)(2,1)S(1)}, bf16[256,128]{0,1:T(8,128)(2,1)S(1)}, u32[]{:S(2)}, u32[]{:S(2)}) %collective-permute-start.2) | collective-permute-done | bytes 65568 | tf_op jit(solution)/shard_map/ppermute | solution.py:44
  70.3 0.0 collective-permute-start.3
  70.3 0.6 constant_dynamic-update-slice_fusion.13
  71.0 5.8 %collective-permute-done.3 = bf16[256,128]{0,1:T(8,128)(2,1)S(1)} collective-permute-done((bf16[256,128]{0,1:T(8,128)(2,1)S(1)}, bf16[256,128]{0,1:T(8,128)(2,1)S(1)}, u32[]{:S(2)}, u32[]{:S(2)}) %collective-permute-start.3) | collective-permute-done | bytes 65568 | tf_op jit(solution)/shard_map/ppermute | solution.py:44
  76.7 0.0 collective-permute-start.4
  76.7 0.6 constant_dynamic-update-slice_fusion.12
  77.3 5.8 %collective-permute-done.4 = bf16[256,128]{0,1:T(8,128)(2,1)S(1)} collective-permute-done((bf16[256,128]{0,1:T(8,128)(2,1)S(1)}, bf16[256,128]{0,1:T(8,128)(2,1)S(1)}, u32[]{:S(2)}, u32[]{:S(2)}) %collective-permute-start.4) | collective-permute-done | bytes 65568 | tf_op jit(solution)/shard_map/ppermute | solution.py:44
  83.1 0.0 collective-permute-start.5
  83.1 0.6 constant_dynamic-update-slice_fusion.11
  83.7 5.8 %collective-permute-done.5 = bf16[256,128]{0,1:T(8,128)(2,1)S(1)} collective-permute-done((bf16[256,128]{0,1:T(8,128)(2,1)S(1)}, bf16[256,128]{0,1:T(8,128)(2,1)S(1)}, u32[]{:S(2)}, u32[]{:S(2)}) %collective-permute-start.5) | collective-permute-done | bytes 65568 | tf_op jit(solution)/shard_map/ppermute | solution.py:44
  89.5 0.0 collective-permute-start.6
  89.5 0.6 constant_dynamic-update-slice_fusion.10
  90.1 7.0 %collective-permute-done.6 = bf16[256,128]{0,1:T(8,128)(2,1)S(1)} collective-permute-done((bf16[256,128]{0,1:T(8,128)(2,1)S(1)}, bf16[256,128]{0,1:T(8,128)(2,1)S(1)}, u32[]{:S(2)}, u32[]{:S(2)}) %collective-permute-start.6) | collective-permute-done | bytes 65568 | tf_op jit(solution)/shard_map/ppermute | solution.py:44
  97.1 0.0 collective-permute-start.7
  97.1 0.6 constant_dynamic-update-slice_fusion.9
  97.7 7.0 %collective-permute-done.7 = bf16[256,128]{0,1:T(8,128)(2,1)S(1)} collective-permute-done((bf16[256,128]{0,1:T(8,128)(2,1)S(1)}, bf16[256,128]{0,1:T(8,128)(2,1)S(1)}, u32[]{:S(2)}, u32[]{:S(2)}) %collective-permute-start.7) | collective-permute-done | bytes 65568 | tf_op jit(solution)/shard_map/ppermute | solution.py:44
  104.7 0.0 collective-permute-start.8
  104.7 0.6 constant_dynamic-update-slice_fusion.8
  105.3 5.8 %collective-permute-done.8 = bf16[256,128]{0,1:T(8,128)(2,1)S(1)} collective-permute-done((bf16[256,128]{0,1:T(8,128)(2,1)S(1)}, bf16[256,128]{0,1:T(8,128)(2,1)S(1)}, u32[]{:S(2)}, u32[]{:S(2)}) %collective-permute-start.8) | collective-permute-done | bytes 65568 | tf_op jit(solution)/shard_map/ppermute | solution.py:44
  111.1 0.0 collective-permute-start.9
  111.1 0.6 constant_dynamic-update-slice_fusion.7
  111.7 6.9 %collective-permute-done.9 = bf16[256,128]{0,1:T(8,128)(2,1)S(1)} collective-permute-done((bf16[256,128]{0,1:T(8,128)(2,1)S(1)}, bf16[256,128]{0,1:T(8,128)(2,1)S(1)}, u32[]{:S(2)}, u32[]{:S(2)}) %collective-permute-start.9) | collective-permute-done | bytes 65568 | tf_op jit(solution)/shard_map/ppermute | solution.py:44
  118.6 0.0 collective-permute-start.10
  118.6 0.6 constant_dynamic-update-slice_fusion.6
  119.2 6.1 %collective-permute-done.10 = bf16[256,128]{0,1:T(8,128)(2,1)S(1)} collective-permute-done((bf16[256,128]{0,1:T(8,128)(2,1)S(1)}, bf16[256,128]{0,1:T(8,128)(2,1)S(1)}, u32[]{:S(2)}, u32[]{:S(2)}) %collective-permute-start.10) | collective-permute-done | bytes 65568 | tf_op jit(solution)/shard_map/ppermute | solution.py:44
  125.4 0.0 collective-permute-start.11
  125.4 0.6 constant_dynamic-update-slice_fusion.5
  126.0 5.8 %collective-permute-done.11 = bf16[256,128]{0,1:T(8,128)(2,1)S(1)} collective-permute-done((bf16[256,128]{0,1:T(8,128)(2,1)S(1)}, bf16[256,128]{0,1:T(8,128)(2,1)S(1)}, u32[]{:S(2)}, u32[]{:S(2)}) %collective-permute-start.11) | collective-permute-done | bytes 65568 | tf_op jit(solution)/shard_map/ppermute | solution.py:44
  131.7 0.0 collective-permute-start.12
  131.7 0.6 constant_dynamic-update-slice_fusion.4
  132.4 5.8 %collective-permute-done.12 = bf16[256,128]{0,1:T(8,128)(2,1)S(1)} collective-permute-done((bf16[256,128]{0,1:T(8,128)(2,1)S(1)}, bf16[256,128]{0,1:T(8,128)(2,1)S(1)}, u32[]{:S(2)}, u32[]{:S(2)}) %collective-permute-start.12) | collective-permute-done | bytes 65568 | tf_op jit(solution)/shard_map/ppermute | solution.py:44
  138.1 0.0 collective-permute-start.13
  138.1 0.6 constant_dynamic-update-slice_fusion.3
  138.8 5.8 %collective-permute-done.13 = bf16[256,128]{0,1:T(8,128)(2,1)S(1)} collective-permute-done((bf16[256,128]{0,1:T(8,128)(2,1)S(1)}, bf16[256,128]{0,1:T(8,128)(2,1)S(1)}, u32[]{:S(2)}, u32[]{:S(2)}) %collective-permute-start.13) | collective-permute-done | bytes 65568 | tf_op jit(solution)/shard_map/ppermute | solution.py:44
  144.5 0.0 collective-permute-start.14
  144.5 0.6 constant_dynamic-update-slice_fusion.2
  145.2 5.8 %collective-permute-done.14 = bf16[256,128]{0,1:T(8,128)(2,1)S(1)} collective-permute-done((bf16[256,128]{0,1:T(8,128)(2,1)S(1)}, bf16[256,128]{0,1:T(8,128)(2,1)S(1)}, u32[]{:S(2)}, u32[]{:S(2)}) %collective-permute-start.14) | collective-permute-done | bytes 65568 | tf_op jit(solution)/shard_map/ppermute | solution.py:44
  150.9 0.0 collective-permute-start.15
  150.9 0.6 constant_dynamic-update-slice_fusion.1
  151.5 5.8 %collective-permute-done.15 = bf16[256,128]{0,1:T(8,128)(2,1)S(1)} collective-permute-done((bf16[256,128]{0,1:T(8,128)(2,1)S(1)}, bf16[256,128]{0,1:T(8,128)(2,1)S(1)}, u32[]{:S(2)}, u32[]{:S(2)}) %collective-permute-start.15) | collective-permute-done | bytes 65568 | tf_op jit(solution)/shard_map/ppermute | solution.py:44
  157.3 0.6 constant_dynamic-update-slice_fusion
  157.9 0.0 all-reduce.2.cloned.1.call-update
  158.0 29.1 %convolution_convert_fusion = bf16[1,128,4096]{2,0,1:T(2,128)(2,1)S(1)} fusion(bf16[1,255,4096]{2,1,0:T(8,128)(2,1)S(1)} %pad_maximum_fusion, bf16[128,1,4096]{2,0,1:T(8,128)(2,1)} %bitcast.2), kind=kOutput, calls=%fused_computation | convolution fusion | flops 134742016 | bytes 4186112 | tf_op jit(solution)/shard_map/conv_general_dilated | solution.py:15
  187.1 2.1 %copy.52 = bf16[1,128,4096]{2,1,0:T(8,128)(2,1)} copy(bf16[1,128,4096]{2,0,1:T(2,128)(2,1)S(1)} %convolution_convert_fusion) | data formatting | bytes 2097152
  189.2 1.7 copy.53
  (4 shorter events, 0.0 us)
Async XLA Ops:
  7.2 7.6 %copy-start = (bf16[1,128,4096]{2,1,0:T(8,128)(2,1)S(1)}, bf16[1,128,4096]{2,1,0:T(8,128)(2,1)}, u32[]{:S(2)}) copy-start(bf16[1,128,4096]{2,1,0:T(8,128)(2,1)} %param.7) | copy-start | bytes 3145732
  7.2 150.8 %reduce-scatter.2.cloned.1.call-start = ((), (), s32[]{:S(2)}) async-start(), calls=%async_computation.1 | async-start | bytes 2228224 | tf_op jit(solution)/shard_map/reduce_scatter | solution.py:48
  10.0 4.6 %collective-permute-start = (bf16[1,127,4096]{2,1,0:T(8,128)(2,1)S(1)}, bf16[1,127,4096]{2,1,0:T(8,128)(2,1)S(1)}, u32[]{:S(2)}, u32[]{:S(2)}) collective-permute-start(bf16[1,127,4096]{2,1,0:T(8,128)(2,1)S(1)} %bitcast.14), channel_id=1, source_target_pairs={{1,0},{2,1},{3,2},{4,3},{5,4},{6,5},{7,6},{8,7},{9,8},{10,9},{11,1... | collective-permute-start | bytes 3121160 | tf_op jit(solution)/shard_map/ppermute | solution.py:10
  48.3 0.8 copy-start.1
  48.3 140.9 %all-reduce.2.cloned.1.call-start = ((), (), s32[]{:S(2)}) async-start(), calls=%async_computation.2 | async-start | bytes 262144 | tf_op jit(solution)/shard_map/psum | solution.py:51
  49.2 14.7 %collective-permute-start.1 = (bf16[256,128]{0,1:T(8,128)(2,1)S(1)}, bf16[256,128]{0,1:T(8,128)(2,1)S(1)}, u32[]{:S(2)}, u32[]{:S(2)}) collective-permute-start(bf16[256,128]{0,1:T(8,128)(2,1)S(1)} %copy.46), channel_id=1, source_target_pairs={{0,1},{1,2},{2,3},{3,4},{4,5},{5,6},{6,7},{7,8},{8,9},{9,10},{10,1... | collective-permute-start | bytes 196616 | tf_op jit(solution)/shard_map/ppermute | solution.py:44
  63.9 6.4 %collective-permute-start.2 = (bf16[256,128]{0,1:T(8,128)(2,1)S(1)}, bf16[256,128]{0,1:T(8,128)(2,1)S(1)}, u32[]{:S(2)}, u32[]{:S(2)}) collective-permute-start(bf16[256,128]{0,1:T(8,128)(2,1)S(1)} %collective-permute-done.1), channel_id=1, source_target_pairs={{0,1},{1,2},{2,3},{3,4},{4,5},{5,6},{6,7},{7,8},{8,9},{9,10},{10,1... | collective-permute-start | bytes 196616 | tf_op jit(solution)/shard_map/ppermute | solution.py:44
  70.3 6.4 %collective-permute-start.3 = (bf16[256,128]{0,1:T(8,128)(2,1)S(1)}, bf16[256,128]{0,1:T(8,128)(2,1)S(1)}, u32[]{:S(2)}, u32[]{:S(2)}) collective-permute-start(bf16[256,128]{0,1:T(8,128)(2,1)S(1)} %collective-permute-done.2), channel_id=1, source_target_pairs={{0,1},{1,2},{2,3},{3,4},{4,5},{5,6},{6,7},{7,8},{8,9},{9,10},{10,1... | collective-permute-start | bytes 196616 | tf_op jit(solution)/shard_map/ppermute | solution.py:44
  76.7 6.4 %collective-permute-start.4 = (bf16[256,128]{0,1:T(8,128)(2,1)S(1)}, bf16[256,128]{0,1:T(8,128)(2,1)S(1)}, u32[]{:S(2)}, u32[]{:S(2)}) collective-permute-start(bf16[256,128]{0,1:T(8,128)(2,1)S(1)} %collective-permute-done.3), channel_id=1, source_target_pairs={{0,1},{1,2},{2,3},{3,4},{4,5},{5,6},{6,7},{7,8},{8,9},{9,10},{10,1... | collective-permute-start | bytes 196616 | tf_op jit(solution)/shard_map/ppermute | solution.py:44
  83.1 6.4 %collective-permute-start.5 = (bf16[256,128]{0,1:T(8,128)(2,1)S(1)}, bf16[256,128]{0,1:T(8,128)(2,1)S(1)}, u32[]{:S(2)}, u32[]{:S(2)}) collective-permute-start(bf16[256,128]{0,1:T(8,128)(2,1)S(1)} %collective-permute-done.4), channel_id=1, source_target_pairs={{0,1},{1,2},{2,3},{3,4},{4,5},{5,6},{6,7},{7,8},{8,9},{9,10},{10,1... | collective-permute-start | bytes 196616 | tf_op jit(solution)/shard_map/ppermute | solution.py:44
  89.5 7.6 %collective-permute-start.6 = (bf16[256,128]{0,1:T(8,128)(2,1)S(1)}, bf16[256,128]{0,1:T(8,128)(2,1)S(1)}, u32[]{:S(2)}, u32[]{:S(2)}) collective-permute-start(bf16[256,128]{0,1:T(8,128)(2,1)S(1)} %collective-permute-done.5), channel_id=1, source_target_pairs={{0,1},{1,2},{2,3},{3,4},{4,5},{5,6},{6,7},{7,8},{8,9},{9,10},{10,1... | collective-permute-start | bytes 196616 | tf_op jit(solution)/shard_map/ppermute | solution.py:44
  97.1 7.6 %collective-permute-start.7 = (bf16[256,128]{0,1:T(8,128)(2,1)S(1)}, bf16[256,128]{0,1:T(8,128)(2,1)S(1)}, u32[]{:S(2)}, u32[]{:S(2)}) collective-permute-start(bf16[256,128]{0,1:T(8,128)(2,1)S(1)} %collective-permute-done.6), channel_id=1, source_target_pairs={{0,1},{1,2},{2,3},{3,4},{4,5},{5,6},{6,7},{7,8},{8,9},{9,10},{10,1... | collective-permute-start | bytes 196616 | tf_op jit(solution)/shard_map/ppermute | solution.py:44
  104.7 6.4 %collective-permute-start.8 = (bf16[256,128]{0,1:T(8,128)(2,1)S(1)}, bf16[256,128]{0,1:T(8,128)(2,1)S(1)}, u32[]{:S(2)}, u32[]{:S(2)}) collective-permute-start(bf16[256,128]{0,1:T(8,128)(2,1)S(1)} %collective-permute-done.7), channel_id=1, source_target_pairs={{0,1},{1,2},{2,3},{3,4},{4,5},{5,6},{6,7},{7,8},{8,9},{9,10},{10,1... | collective-permute-start | bytes 196616 | tf_op jit(solution)/shard_map/ppermute | solution.py:44
  111.1 7.5 %collective-permute-start.9 = (bf16[256,128]{0,1:T(8,128)(2,1)S(1)}, bf16[256,128]{0,1:T(8,128)(2,1)S(1)}, u32[]{:S(2)}, u32[]{:S(2)}) collective-permute-start(bf16[256,128]{0,1:T(8,128)(2,1)S(1)} %collective-permute-done.8), channel_id=1, source_target_pairs={{0,1},{1,2},{2,3},{3,4},{4,5},{5,6},{6,7},{7,8},{8,9},{9,10},{10,1... | collective-permute-start | bytes 196616 | tf_op jit(solution)/shard_map/ppermute | solution.py:44
  118.6 6.8 %collective-permute-start.10 = (bf16[256,128]{0,1:T(8,128)(2,1)S(1)}, bf16[256,128]{0,1:T(8,128)(2,1)S(1)}, u32[]{:S(2)}, u32[]{:S(2)}) collective-permute-start(bf16[256,128]{0,1:T(8,128)(2,1)S(1)} %collective-permute-done.9), channel_id=1, source_target_pairs={{0,1},{1,2},{2,3},{3,4},{4,5},{5,6},{6,7},{7,8},{8,9},{9,10},{10,1... | collective-permute-start | bytes 196616 | tf_op jit(solution)/shard_map/ppermute | solution.py:44
  125.4 6.4 %collective-permute-start.11 = (bf16[256,128]{0,1:T(8,128)(2,1)S(1)}, bf16[256,128]{0,1:T(8,128)(2,1)S(1)}, u32[]{:S(2)}, u32[]{:S(2)}) collective-permute-start(bf16[256,128]{0,1:T(8,128)(2,1)S(1)} %collective-permute-done.10), channel_id=1, source_target_pairs={{0,1},{1,2},{2,3},{3,4},{4,5},{5,6},{6,7},{7,8},{8,9},{9,10},{10,1... | collective-permute-start | bytes 196616 | tf_op jit(solution)/shard_map/ppermute | solution.py:44
  131.7 6.4 %collective-permute-start.12 = (bf16[256,128]{0,1:T(8,128)(2,1)S(1)}, bf16[256,128]{0,1:T(8,128)(2,1)S(1)}, u32[]{:S(2)}, u32[]{:S(2)}) collective-permute-start(bf16[256,128]{0,1:T(8,128)(2,1)S(1)} %collective-permute-done.11), channel_id=1, source_target_pairs={{0,1},{1,2},{2,3},{3,4},{4,5},{5,6},{6,7},{7,8},{8,9},{9,10},{10,1... | collective-permute-start | bytes 196616 | tf_op jit(solution)/shard_map/ppermute | solution.py:44
  138.1 6.4 %collective-permute-start.13 = (bf16[256,128]{0,1:T(8,128)(2,1)S(1)}, bf16[256,128]{0,1:T(8,128)(2,1)S(1)}, u32[]{:S(2)}, u32[]{:S(2)}) collective-permute-start(bf16[256,128]{0,1:T(8,128)(2,1)S(1)} %collective-permute-done.12), channel_id=1, source_target_pairs={{0,1},{1,2},{2,3},{3,4},{4,5},{5,6},{6,7},{7,8},{8,9},{9,10},{10,1... | collective-permute-start | bytes 196616 | tf_op jit(solution)/shard_map/ppermute | solution.py:44
  144.5 6.4 %collective-permute-start.14 = (bf16[256,128]{0,1:T(8,128)(2,1)S(1)}, bf16[256,128]{0,1:T(8,128)(2,1)S(1)}, u32[]{:S(2)}, u32[]{:S(2)}) collective-permute-start(bf16[256,128]{0,1:T(8,128)(2,1)S(1)} %collective-permute-done.13), channel_id=1, source_target_pairs={{0,1},{1,2},{2,3},{3,4},{4,5},{5,6},{6,7},{7,8},{8,9},{9,10},{10,1... | collective-permute-start | bytes 196616 | tf_op jit(solution)/shard_map/ppermute | solution.py:44
  150.9 6.4 %collective-permute-start.15 = (bf16[256,128]{0,1:T(8,128)(2,1)S(1)}, bf16[256,128]{0,1:T(8,128)(2,1)S(1)}, u32[]{:S(2)}, u32[]{:S(2)}) collective-permute-start(bf16[256,128]{0,1:T(8,128)(2,1)S(1)} %collective-permute-done.14), channel_id=1, source_target_pairs={{0,1},{1,2},{2,3},{3,4},{4,5},{5,6},{6,7},{7,8},{8,9},{9,10},{10,1... | collective-permute-start | bytes 196616 | tf_op jit(solution)/shard_map/ppermute | solution.py:44
Sparse Core Ops, SparseCore 0:
  48.4 76.1 reduce-scatter.1
  158.1 18.6 all-reduce.1
